TPU v7x, 512 devices: a whole 4x4x16 slice. The times are simulated.
512 devices in a mesh: rx: 64 (over z_lo, x, core), band: 8 (over y, z_hi).
Axes of the slice: x: 4, y: 4, z: 16 (z_hi: 2, z_lo: 8; z = z_hi * 8 + z_lo), core: 2. Of those that a mesh axis runs over, the one named last changes fastest.
Arguments:
- spectra: bfloat16 [2, 256, 64, 8192], P(None, 'band', None, 'rx'), may hold values from -6 to 6
- source_index: int32 [64], replicated, may hold values from 0 to 8191, as said below
Outputs:
- stack: bfloat16 [2, 256, 64, 8192], P(None, 'band', None, 'rx')
Inputs may be any that keep to these rules, and one draw needn't show every extreme that they name: `source_index`: virtual source s is one of channels s * 128 to (s + 1) * 128 - 1; the first and the last channel are sources.
All inputs are finite; a program needn't handle non-finite values.
Results may differ from a plain program's by a relative error of at most 0.0059.
Values may be sent and summed in bfloat16 or wider, within the bound.
A program may use at most 64 MiB of HBM per device.

v0:
```python
import jax
import jax.numpy as jnp
from jax import lax
from jax.sharding import PartitionSpec as P

HALF = 4


def padded_2(block, sides, width):
    for axis, dim in sides:
        count = lax.axis_size(axis)
        forward = [(i, i + 1) for i in range(count - 1)]
        backward = [(target, source) for source, target in forward]
        low = lax.ppermute(
            lax.slice_in_dim(block, block.shape[dim] - width, None, axis=dim), axis, forward
        )
        high = lax.ppermute(lax.slice_in_dim(block, 0, width, axis=dim), axis, backward)
        block = jnp.concatenate([low, block, high], axis=dim)
    return block


def magnitude(values_in):
    values = values_in.astype(jnp.float32)
    rounded = lax.optimization_barrier(
        jnp.sqrt(values[0] * values[0] + values[1] * values[1]).astype(jnp.bfloat16)
    )
    return rounded


def whiten(spectra):
    bin_count = spectra.shape[1]
    padded = padded_2(spectra, (("band", 1),), HALF)
    amplitude = magnitude(padded).astype(jnp.float32)
    total = amplitude[0:bin_count]
    for offset in range(1, 2 * HALF + 1):
        total = total + amplitude[offset : offset + bin_count]
    smooth = total / (2 * HALF + 1)
    return (spectra.astype(jnp.float32) / (smooth + 0.1)[None]).astype(jnp.bfloat16)


def cross_spectra(whitened, source_rows):
    bin_count = whitened.shape[1]
    window_count = whitened.shape[2]
    sources = source_rows.reshape(source_rows.shape[0], 2, bin_count, window_count)
    source_real = sources[:, 0]
    source_imag = sources[:, 1]
    coefficients = jnp.stack(
        [jnp.stack([source_real, source_imag], 0), jnp.stack([-source_imag, source_real], 0)], 0
    )
    products = jnp.einsum(
        "oqnfw,qfwc->ofnc", coefficients, whitened, preferred_element_type=jnp.float32
    )
    return (products / window_count).astype(jnp.bfloat16)


def local(spectra, source_index):
    whitened = whiten(spectra)
    device_rank = lax.axis_index("rx")
    channels_here = spectra.shape[3]
    local_column = source_index[device_rank] - device_rank * channels_here
    own_row = lax.dynamic_slice_in_dim(whitened, local_column, 1, 3).reshape(1, -1)
    collected = lax.all_gather(own_row, "rx", axis=0, tiled=True)
    return cross_spectra(whitened, collected)


def solution(mesh):
    return jax.shard_map(
        local,
        mesh=mesh,
        in_specs=(P(None, "band", None, "rx"), P()),
        out_specs=P(None, "band", None, "rx"),
        check_vma=False,
    )
```

profile of v0, /device:TPU:1, one launch (start us, length us, event | category | flops | bytes accessed | tf_op | source)
XLA Modules:
  0.0 172.9 jit_solution(2140125977759759294)
XLA Ops:
  0.0 1.0 fusion.20
  1.0 16.3 %collective-permute-start = (bf16[2,4,64,128]{3,2,1,0:T(8,128)(2,1)S(1)}, bf16[2,4,64,128]{3,2,1,0:T(8,128)(2,1)S(1)}, u32[]{:S(2)}, u32[]{:S(2)}) collective-permute-start(bf16[2,4,64,128]{3,2,1,0:T(8,128)(2,1)S(1)} %get-tuple-element.7), channel_id=1, source_target_pairs={{0,1},{1,2},{2,3},{3,4},{4,5},{5,6},{6,7},{8,9},{9,10},{10,11},{11... | collective-permute-start | bytes 393224 | tf_op jit(solution)/shard_map/ppermute | solution.py:14
  17.3 1.3 collective-permute-start.1
  18.6 1.2 dynamic_slice.6
  20.5 0.0 collective-permute-done
  20.5 16.2 %collective-permute-done.1 = bf16[2,4,64,128]{3,2,1,0:T(8,128)(2,1)S(1)} collective-permute-done((bf16[2,4,64,128]{3,2,1,0:T(8,128)(2,1)S(1)}, bf16[2,4,64,128]{3,2,1,0:T(8,128)(2,1)S(1)}, u32[]{:S(2)}, u32[]{:S(2)}) %collective-permute-start.1) | collective-permute-done | bytes 131104 | tf_op jit(solution)/shard_map/ppermute | solution.py:17
  36.7 1.4 maximum_convert_fusion
  38.1 0.5 fusion.16
  38.6 0.1 convert_element_type.28
  38.7 0.0 copy-start
  38.7 0.3 fusion.14
  39.1 0.9 copy-done
  40.0 0.3 divide_convert_fusion
  40.3 0.9 dynamic-slice_reduce_fusion
  41.2 0.1 reshape.24
  41.3 122.3 %all-gather = bf16[64,1,4096]{2,1,0:T(2,128)(2,1)S(1)} all-gather(bf16[1,1,4096]{2,1,0:T(2,128)(2,1)S(1)} %reshape.24), channel_id=1, replica_groups=mesh['rx'=64,'band'=8] {'rx'}, dimensions={0}, use_global_device_ids=true | all-gather | bytes 532480 | tf_op jit(solution)/shard_map/all_gather | solution.py:62
  163.7 3.9 %reduce.1 = bf16[64,4096]{1,0:T(8,128)(2,1)} reduce(bf16[64,1,4096]{2,1,0:T(2,128)(2,1)S(1)} %all-gather, bf16[]{:T(256)} %constant.20), dimensions={1}, to_apply=%all-gather.reduce_sub_computation | reduce | bytes 1048578 | tf_op jit(solution)/shard_map/all_gather | solution.py:62
  167.6 2.1 %reshape.23 = bf16[64,2,32,64]{3,2,1,0:T(8,128)(2,1)S(1)} reshape(bf16[64,4096]{1,0:T(8,128)(2,1)} %reduce.1) | data formatting | bytes 1048576 | tf_op jit(solution)/shard_map/reshape | solution.py:44
  169.7 0.1 fusion.19
  169.7 0.2 fusion.18
  170.0 0.4 copy_bitcast_fusion
  170.4 0.4 maximum_bitcast_fusion
  170.8 1.0 fusion.7
  171.8 1.1 copy.15
Async XLA Ops:
  1.0 19.5 %collective-permute-start = (bf16[2,4,64,128]{3,2,1,0:T(8,128)(2,1)S(1)}, bf16[2,4,64,128]{3,2,1,0:T(8,128)(2,1)S(1)}, u32[]{:S(2)}, u32[]{:S(2)}) collective-permute-start(bf16[2,4,64,128]{3,2,1,0:T(8,128)(2,1)S(1)} %get-tuple-element.7), channel_id=1, source_target_pairs={{0,1},{1,2},{2,3},{3,4},{4,5},{5,6},{6,7},{8,9},{9,10},{10,11},{11... | collective-permute-start | bytes 393224 | tf_op jit(solution)/shard_map/ppermute | solution.py:14
  17.3 19.4 %collective-permute-start.1 = (bf16[2,4,64,128]{3,2,1,0:T(8,128)(2,1)S(1)}, bf16[2,4,64,128]{3,2,1,0:T(8,128)(2,1)S(1)}, u32[]{:S(2)}, u32[]{:S(2)}) collective-permute-start(bf16[2,4,64,128]{3,2,1,0:T(8,128)(2,1)S(1)} %get-tuple-element.8), channel_id=1, source_target_pairs={{1,0},{2,1},{3,2},{4,3},{5,4},{6,5},{7,6},{9,8},{10,9},{11,10},{12... | collective-permute-start | bytes 393224 | tf_op jit(solution)/shard_map/ppermute | solution.py:17
  38.7 1.2 copy-start
where the time goes:
time: 176 us; the launch traced here: 173 us
  blocking collectives  122 us (69%)
  starting transfers between devices  17.6 us (10%)
  waiting for transfers between devices  16.2 us (9%)
  local copies, waits for them, and re-layouts  7.71 us (4%)
  other arithmetic  7.3 us (4%)
    all_gather x1, blocking collectives, local(): collected = lax.all_gather(own_row, 'rx', axis=0, tiled=True)  122 us
    ppermute x1, starting transfers between devices, padded_2(): lax.ppermute(lax.slice_in_dim(block, block.shape[dim] - width, None, axis...  16.3 us
    ppermute x1, waiting for transfers between devices, padded_2(): lax.ppermute(lax.slice_in_dim(block, 0, width, axis=dim), axis, backward)  16.2 us
    all_gather x1, other arithmetic, local(): collected = lax.all_gather(own_row, 'rx', axis=0, tiled=True)  3.94 us
  transfers between devices with their start and end apart: 2, of which 1 were waited for; matrix products, arithmetic and copies ran while one was open for 1% of the time, Pallas kernels for 0%

commit v1 on v0

v1 whole, which is shorter than its diff:
```python
import functools

import jax
import jax.numpy as jnp
from jax import lax
from jax.experimental import pallas as pl
from jax.experimental.pallas import tpu as pltpu
from jax.sharding import PartitionSpec as P

HALF = 4
BINS = 32
WIN = 64
CH = 128
ROWS = 8
COLS = 8
BANDS = 8
MESH = pl.DeviceIdType.MESH


def gather_kernel(src_ref, x_ref, g_ref, rows, edge_out, edge_in,
                  zs, zr, es, er, js, jr):
    rx = lax.axis_index("rx")
    band = lax.axis_index("band")
    z = lax.div(rx, COLS)
    j = lax.rem(rx, COLS)
    above = lax.rem(band + 1, BANDS)
    below = lax.rem(band + BANDS - 1, BANDS)

    def along_z(d):
        return lax.rem(z + d, ROWS)

    def along_j(d):
        return lax.rem(j + d, COLS)

    barrier = pltpu.get_barrier_semaphore()
    for d in range(1, ROWS):
        pl.semaphore_signal(barrier, inc=1, device_id=(along_z(d) * COLS + j, band), device_id_type=MESH)
    for d in range(1, COLS):
        pl.semaphore_signal(barrier, inc=1, device_id=(z * COLS + along_j(d), band), device_id_type=MESH)
    for d in range(ROWS):
        for other in (above, below):
            pl.semaphore_signal(barrier, inc=1, device_id=(along_z(d) * COLS + j, other), device_id_type=MESH)

    column = src_ref[rx] - rx * CH
    lane = lax.broadcasted_iota(jnp.int32, (BINS, CH), 1)
    bin_row = lax.broadcasted_iota(jnp.int32, (BINS, CH), 0)
    pick = jnp.where(lane == column, 1.0, 0.0).astype(jnp.float32)
    row = jnp.zeros((BINS, CH), jnp.float32)
    for f in range(BINS):
        one = jnp.where(bin_row == f, pick, 0.0).astype(jnp.bfloat16)
        both = x_ref[:, f].reshape(2 * WIN, CH)
        row = row + lax.dot_general(one, both, (((1,), (1,)), ((), ())),
                                    preferred_element_type=jnp.float32)

    def amplitude(values):
        square = values * values
        return jnp.sqrt(square + pltpu.roll(square, WIN, 1)).astype(jnp.bfloat16).astype(jnp.float32)

    own_amp = amplitude(row)
    edge_out[0] = own_amp[0:HALF]
    edge_out[1] = own_amp[BINS - HALF:BINS]
    rows[z] = row.astype(jnp.bfloat16)

    pl.semaphore_wait(barrier, (ROWS - 1) + (COLS - 1) + 2 * ROWS)

    def edge_copy(side, d, slot):
        other = below if side == 0 else above
        return pltpu.make_async_remote_copy(
            src_ref=edge_out.at[side], dst_ref=edge_in.at[1 - side, slot],
            send_sem=es.at[side, d], recv_sem=er.at[side, d],
            device_id=(along_z(d) * COLS + j, other), device_id_type=MESH)

    def row_copy(d, slot):
        return pltpu.make_async_remote_copy(
            src_ref=rows.at[z], dst_ref=rows.at[slot],
            send_sem=zs.at[d], recv_sem=zr.at[d],
            device_id=(along_z(d) * COLS + j, band), device_id_type=MESH)

    for d in (4, 3, 5, 2, 6, 1, 7, 0):
        for side in range(2):
            edge_copy(side, d, z).start()
    for d in (7, 6, 5, 4, 3, 2, 1):
        row_copy(d, z).start()
    for d in range(1, ROWS):
        row_copy(d, lax.rem(z - d + ROWS, ROWS)).wait_recv()
    for d in range(ROWS):
        for side in range(2):
            edge_copy(side, d, lax.rem(z - d + ROWS, ROWS)).wait_recv()

    has_low = (band > 0).astype(jnp.float32)
    has_high = (band < BANDS - 1).astype(jnp.float32)
    for k in range(ROWS):
        values = rows[k].astype(jnp.float32)
        padded = jnp.concatenate(
            [edge_in[0, k] * has_low, amplitude(values), edge_in[1, k] * has_high], axis=0)
        total = padded[0:BINS]
        for offset in range(1, 2 * HALF + 1):
            total = total + padded[offset:offset + BINS]
        smooth = total / (2 * HALF + 1)
        g_ref[j, k] = (values / (smooth + 0.1)).astype(jnp.bfloat16)

    def block_copy(d, slot):
        return pltpu.make_async_remote_copy(
            src_ref=g_ref.at[j], dst_ref=g_ref.at[slot],
            send_sem=js.at[d], recv_sem=jr.at[d],
            device_id=(z * COLS + along_j(d), band), device_id_type=MESH)

    for d in (4, 3, 5, 2, 6, 1, 7):
        block_copy(d, j).start()
    for d in range(1, ROWS):
        row_copy(d, z).wait_send()
    for d in range(ROWS):
        for side in range(2):
            edge_copy(side, d, z).wait_send()
    for d in range(1, COLS):
        block_copy(d, lax.rem(j - d + COLS, COLS)).wait_recv()
    for d in range(1, COLS):
        block_copy(d, j).wait_send()


def stack_kernel(x_ref, low_ref, high_ref, g_ref, out_ref, source, amp):
    for k in range(ROWS):
        for j in range(COLS):
            source[pl.ds((k * COLS + j) * BINS, BINS), :] = g_ref[j, k].astype(jnp.float32)
    amp[0:HALF] = low_ref[...].astype(jnp.float32)
    amp[BINS + HALF:BINS + 2 * HALF] = high_ref[...].astype(jnp.float32)
    for f in range(BINS):
        real = x_ref[0, f].astype(jnp.float32)
        imag = x_ref[1, f].astype(jnp.float32)
        amp[HALF + f] = jnp.sqrt(real * real + imag * imag).astype(jnp.bfloat16).astype(jnp.float32)
    lane = lax.broadcasted_iota(jnp.int32, (ROWS * COLS, 2 * WIN), 1)
    for f in range(BINS):
        total = amp[f]
        for offset in range(1, 2 * HALF + 1):
            total = total + amp[f + offset]
        smooth = total / (2 * HALF + 1)
        scale = 1.0 / (smooth + 0.1)
        white = jnp.concatenate(
            [(x_ref[q, f].astype(jnp.float32) * scale).astype(jnp.bfloat16) for q in range(2)], axis=0)
        picked = source[pl.ds(f, ROWS * COLS, stride=BINS), :]
        turned = pltpu.roll(picked, WIN, 1)
        turned = jnp.where(lane < WIN, -turned, turned)
        left = jnp.concatenate([picked.astype(jnp.bfloat16), turned.astype(jnp.bfloat16)], axis=0)
        product = jnp.dot(left, white, preferred_element_type=jnp.float32) * (1.0 / WIN)
        out_ref[0, f] = product[0:WIN].astype(jnp.bfloat16)
        out_ref[1, f] = product[WIN:2 * WIN].astype(jnp.bfloat16)


def edge_amplitude(part):
    values = part.astype(jnp.float32)
    return jnp.sqrt(values[0] * values[0] + values[1] * values[1]).astype(jnp.bfloat16)


def local(spectra, source_index):
    forward = [(i, i + 1) for i in range(BANDS - 1)]
    backward = [(t, s) for s, t in forward]
    low = lax.ppermute(edge_amplitude(spectra[:, BINS - HALF:]), "band", forward)
    high = lax.ppermute(edge_amplitude(spectra[:, :HALF]), "band", backward)
    vmem = pl.BlockSpec(memory_space=pltpu.VMEM)
    rows = pl.pallas_call(
        gather_kernel,
        out_shape=jax.ShapeDtypeStruct((COLS, ROWS, BINS, 2 * WIN), jnp.bfloat16),
        in_specs=[pl.BlockSpec(memory_space=pltpu.SMEM), vmem],
        out_specs=vmem,
        scratch_shapes=[
            pltpu.VMEM((ROWS, BINS, 2 * WIN), jnp.bfloat16),
            pltpu.VMEM((2, HALF, 2 * WIN), jnp.float32),
            pltpu.VMEM((2, ROWS, HALF, 2 * WIN), jnp.float32),
            pltpu.SemaphoreType.DMA((ROWS,)),
            pltpu.SemaphoreType.DMA((ROWS,)),
            pltpu.SemaphoreType.DMA((2, ROWS)),
            pltpu.SemaphoreType.DMA((2, ROWS)),
            pltpu.SemaphoreType.DMA((COLS,)),
            pltpu.SemaphoreType.DMA((COLS,)),
        ],
        compiler_params=pltpu.CompilerParams(collective_id=0, has_side_effects=True),
        cost_estimate=pl.CostEstimate(flops=40_000_000, bytes_accessed=40_000_000, transcendentals=0),
        name="source_rows",
    )(source_index, spectra)
    return pl.pallas_call(
        stack_kernel,
        out_shape=jax.ShapeDtypeStruct((2, BINS, ROWS * COLS, CH), jnp.bfloat16),
        in_specs=[vmem] * 4,
        out_specs=vmem,
        scratch_shapes=[
            pltpu.VMEM((ROWS * COLS * BINS, 2 * WIN), jnp.float32),
            pltpu.VMEM((BINS + 2 * HALF, WIN, CH), jnp.float32),
        ],
        name="stack",
    )(spectra, low, high, rows)


def solution(mesh):
    return jax.shard_map(
        local,
        mesh=mesh,
        in_specs=(P(None, "band", None, "rx"), P()),
        out_specs=P(None, "band", None, "rx"),
        check_vma=False,
    )
```

time: 176 us -> 56.1 us (0.32); the launches traced: 173 us -> 55.9 us
  blocking collectives: 122 us -> 0 us
  Pallas kernels: 0 us -> 35.9 us
  waiting for transfers between devices: 16.2 us -> 0.01 us
  local copies, waits for them, and re-layouts: 7.71 us -> 1.23 us
  other arithmetic: 7.3 us -> 1.11 us
    all_gather x1 -> x0, blocking collectives: 122 us -> none  [local(): collected = lax.all_gather(own_row, 'rx', axis=0, tiled=True)]
    pallas_call x0 -> x2, Pallas kernels: none -> 35.9 us  [the longest x1 31.7 us: local(): pl.pallas_call(gather_kernel, out_shape=jax.ShapeDtypeStruct((COLS, ROWS,...]
    ppermute x2, waiting for transfers between devices: 16.2 us -> 0.01 us  [the longest x1 0.01 us: local(): lax.ppermute(edge_amplitude(spectra[:, BINS - HALF:]), 'band', forward)]
    all_gather x1 -> x0, other arithmetic: 3.94 us -> none  [local(): collected = lax.all_gather(own_row, 'rx', axis=0, tiled=True)]
    dynamic_slice x2 -> x0, local copies, waits for them, and re-layouts: 2.18 us -> none  [the longest x1 1.24 us: local(): local_column = source_index[device_rank] - device_rank * channels_here]
    reshape x1 -> x0, local copies, waits for them, and re-layouts: 2.05 us -> none  [cross_spectra(): source_rows.reshape(source_rows.shape[0], 2, bin_count, window_count)]
  transfers between devices with their start and end apart: 2 -> 2, of which waited for: 1 -> 0; matrix products, arithmetic and copies ran while one was open for 1% -> 0% of each run, Pallas kernels for 0% -> 57%
where the time goes in v1:
time: 56.1 us; the launch traced here: 55.9 us
  Pallas kernels  35.9 us (64%)
  starting transfers between devices  17.6 us (31%)
  local copies, waits for them, and re-layouts  1.23 us (2%)
  other arithmetic  1.11 us (2%)
    pallas_call x1, Pallas kernels, local(): pl.pallas_call(gather_kernel, out_shape=jax.ShapeDtypeStruct((COLS, ROWS,...  31.7 us
    ppermute x1, starting transfers between devices, local(): lax.ppermute(edge_amplitude(spectra[:, BINS - HALF:]), 'band', forward)  16.3 us
    pallas_call x1, Pallas kernels, local(): pl.pallas_call(stack_kernel, out_shape=jax.ShapeDtypeStruct((2, BINS, ROW...  4.2 us
    ppermute x1, starting transfers between devices, local(): high = lax.ppermute(edge_amplitude(spectra[:, :HALF]), 'band', backward)  1.29 us
    unnamed x4, local copies, waits for them, and re-layouts  1.23 us
  transfers between devices with their start and end apart: 2, of which 0 were waited for; matrix products, arithmetic and copies ran while one was open for 0% of the time, Pallas kernels for 57%

profile of v1, /device:TPU:1, one launch (start us, length us, event | category | flops | bytes accessed | tf_op | source)
XLA Modules:
  0.0 55.9 jit_solution(1942487560956743826)
XLA Ops:
  0.0 1.0 %slice_convert_fusion = (f32[2,4,64,128]{3,2,1,0:T(8,128)S(1)}, f32[2,4,64,128]{3,2,1,0:T(8,128)S(1)}) fusion(bf16[2,32,64,128]{3,2,1,0:T(8,128)(2,1)} %x_ref.3), kind=kLoop, calls=%fused_computation.10 | loop fusion | flops 131072 | bytes 786432 | tf_op jit(solution)/shard_map/convert_element_type | solution.py:150
  1.0 0.1 fusion.6
  1.1 16.3 %collective-permute-start = (bf16[4,64,128]{2,1,0:T(8,128)(2,1)S(1)}, bf16[4,64,128]{2,1,0:T(8,128)(2,1)S(1)}, u32[]{:S(2)}, u32[]{:S(2)}) collective-permute-start(bf16[4,64,128]{2,1,0:T(8,128)(2,1)S(1)} %fusion.6), channel_id=1, source_target_pairs={{0,1},{1,2},{2,3},{3,4},{4,5},{5,6},{6,7},{8,9},{9,10},{10,11},{11... | collective-permute-start | bytes 196616 | tf_op jit(solution)/shard_map/ppermute | solution.py:157
  17.3 0.1 fusion.7
  17.4 1.3 %collective-permute-start.1 = (bf16[4,64,128]{2,1,0:T(8,128)(2,1)S(1)}, bf16[4,64,128]{2,1,0:T(8,128)(2,1)S(1)}, u32[]{:S(2)}, u32[]{:S(2)}) collective-permute-start(bf16[4,64,128]{2,1,0:T(8,128)(2,1)S(1)} %fusion.7), channel_id=1, source_target_pairs={{1,0},{2,1},{3,2},{4,3},{5,4},{6,5},{7,6},{9,8},{10,9},{11,10},{12... | collective-permute-start | bytes 196616 | tf_op jit(solution)/shard_map/ppermute | solution.py:158
  18.7 31.7 %source_rows.1.g_ref = bf16[8,8,32,128]{3,2,1,0:T(8,128)(2,1)} custom-call(s32[64]{0:T(128)} %src_ref.1, bf16[2,32,64,128]{3,2,1,0:T(8,128)(2,1)} %x_ref.3), custom_call_target="tpu_custom_call" | custom-call | flops 40000000 | bytes 40000000 | tf_op jit(solution)/shard_map/source_rows/pallas_call | solution.py:160
  50.5 0.0 collective-permute-done.low_ref
  50.5 0.0 copy-start
  50.5 0.0 collective-permute-done.1.high_ref
  50.5 0.6 %copy-done = bf16[4,64,128]{2,1,0:T(8,128)(2,1)} copy-done((bf16[4,64,128]{2,1,0:T(8,128)(2,1)}, bf16[4,64,128]{2,1,0:T(8,128)(2,1)S(1)}, u32[]{:S(2)}) %copy-start) | copy-done | bytes 65560
  51.1 0.0 copy-start.1
  51.1 0.6 %copy-done.1 = bf16[4,64,128]{2,1,0:T(8,128)(2,1)} copy-done((bf16[4,64,128]{2,1,0:T(8,128)(2,1)}, bf16[4,64,128]{2,1,0:T(8,128)(2,1)S(1)}, u32[]{:S(2)}) %copy-start.1) | copy-done | bytes 65560
  51.7 4.2 %stack.1 = bf16[2,32,64,128]{3,2,1,0:T(8,128)(2,1)} custom-call(bf16[2,32,64,128]{3,2,1,0:T(8,128)(2,1)} %x_ref.3, bf16[4,64,128]{2,1,0:T(8,128)(2,1)} %copy-done, bf16[4,64,128]{2,1,0:T(8,128)(2,1)} %copy-done.1, bf16[8,8,32,128]{3,2,1,0:T(8,128)(2,1)} %source_rows.1.g_ref), custom_call_target="tpu_custom_call" | custom-call | tf_op jit(solution)/shard_map/stack/pallas_call | solution.py:180
Async XLA Ops:
  1.1 49.4 %collective-permute-start = (bf16[4,64,128]{2,1,0:T(8,128)(2,1)S(1)}, bf16[4,64,128]{2,1,0:T(8,128)(2,1)S(1)}, u32[]{:S(2)}, u32[]{:S(2)}) collective-permute-start(bf16[4,64,128]{2,1,0:T(8,128)(2,1)S(1)} %fusion.6), channel_id=1, source_target_pairs={{0,1},{1,2},{2,3},{3,4},{4,5},{5,6},{6,7},{8,9},{9,10},{10,11},{11... | collective-permute-start | bytes 196616 | tf_op jit(solution)/shard_map/ppermute | solution.py:157
  17.4 33.1 %collective-permute-start.1 = (bf16[4,64,128]{2,1,0:T(8,128)(2,1)S(1)}, bf16[4,64,128]{2,1,0:T(8,128)(2,1)S(1)}, u32[]{:S(2)}, u32[]{:S(2)}) collective-permute-start(bf16[4,64,128]{2,1,0:T(8,128)(2,1)S(1)} %fusion.7), channel_id=1, source_target_pairs={{1,0},{2,1},{3,2},{4,3},{5,4},{6,5},{7,6},{9,8},{10,9},{11,10},{12... | collective-permute-start | bytes 196616 | tf_op jit(solution)/shard_map/ppermute | solution.py:158
  50.5 0.6 %copy-start = (bf16[4,64,128]{2,1,0:T(8,128)(2,1)}, bf16[4,64,128]{2,1,0:T(8,128)(2,1)S(1)}, u32[]{:S(2)}) copy-start(bf16[4,64,128]{2,1,0:T(8,128)(2,1)S(1)} %collective-permute-done.low_ref) | copy-start | bytes 196612
  51.1 0.6 %copy-start.1 = (bf16[4,64,128]{2,1,0:T(8,128)(2,1)}, bf16[4,64,128]{2,1,0:T(8,128)(2,1)S(1)}, u32[]{:S(2)}) copy-start(bf16[4,64,128]{2,1,0:T(8,128)(2,1)S(1)} %collective-permute-done.1.high_ref) | copy-start | bytes 196612

commit v2 on v1

v2 whole, which is shorter than its diff:
```python
import functools

import jax
import jax.numpy as jnp
from jax import lax
from jax.experimental import pallas as pl
from jax.experimental.pallas import tpu as pltpu
from jax.sharding import PartitionSpec as P

HALF = 4
BINS = 32
WIN = 64
CH = 128
ROWS = 8
COLS = 8
BANDS = 8
MESH = pl.DeviceIdType.MESH


def rounded_amplitude(real, imag):
    return jnp.sqrt(real * real + imag * imag).astype(jnp.bfloat16)


def whiten_four(x, amp, white, first):
    a = [amp[first + k] for k in range(4 + 2 * HALF)]
    common = ((a[3] + a[4]) + (a[5] + a[6])) + (a[7] + a[8])
    early = a[1] + a[2]
    late = a[9] + a[10]
    sides = (a[0] + early, early + a[9], a[2] + late, late + a[11])
    for k in range(4):
        smooth = (common + sides[k]) / (2 * HALF + 1)
        scale = 1.0 / (smooth + 0.1)
        for q in range(2):
            white[first + k, q * WIN:(q + 1) * WIN] = (
                x[q, first + k].astype(jnp.float32) * scale).astype(jnp.bfloat16)


def coefficients(source, f):
    lane = lax.broadcasted_iota(jnp.int32, (ROWS * COLS, 2 * WIN), 1)
    picked = source[pl.ds(f, ROWS * COLS, stride=BINS), :]
    turned = pltpu.roll(picked, WIN, 1)
    turned = jnp.where(lane < WIN, -turned, turned)
    return jnp.concatenate([picked.astype(jnp.bfloat16), turned.astype(jnp.bfloat16)], axis=0)


def multiply(left, white, out, f):
    product = jnp.dot(left, white[f], preferred_element_type=jnp.float32) * (1.0 / WIN)
    out[0, f] = product[0:WIN].astype(jnp.bfloat16)
    out[1, f] = product[WIN:2 * WIN].astype(jnp.bfloat16)


def correlate_kernel(src_ref, x_hbm, out_ref, x, amp, white, source, left, halo_out, halo_in,
                     rows, edge_out, edge_in, blocks, xs, zs, zr, es, er, js, jr, hs, hr):
    rx = lax.axis_index("rx")
    band = lax.axis_index("band")
    z = lax.div(rx, COLS)
    j = lax.rem(rx, COLS)
    above = lax.rem(band + 1, BANDS)
    below = lax.rem(band + BANDS - 1, BANDS)

    def along_z(d):
        return lax.rem(z + d, ROWS)

    def along_j(d):
        return lax.rem(j + d, COLS)

    barrier = pltpu.get_barrier_semaphore()
    for d in range(ROWS):
        for other in (above, below):
            pl.semaphore_signal(barrier, inc=1, device_id=(along_z(d) * COLS + j, other), device_id_type=MESH)
    for d in range(1, ROWS):
        pl.semaphore_signal(barrier, inc=1, device_id=(along_z(d) * COLS + j, band), device_id_type=MESH)
    for d in range(1, COLS):
        pl.semaphore_signal(barrier, inc=1, device_id=(z * COLS + along_j(d), band), device_id_type=MESH)

    load = pltpu.make_async_copy(x_hbm, x, xs)
    load.start()
    load.wait()

    for k in range(HALF):
        for side, f in ((0, k), (1, BINS - HALF + k)):
            value = rounded_amplitude(x[0, f].astype(jnp.float32), x[1, f].astype(jnp.float32))
            halo_out[side, k] = value
            amp[HALF + f] = value.astype(jnp.float32)

    column = src_ref[rx] - rx * CH
    lane = lax.broadcasted_iota(jnp.int32, (BINS, CH), 1)
    bin_row = lax.broadcasted_iota(jnp.int32, (BINS, CH), 0)
    pick = jnp.where(lane == column, 1.0, 0.0).astype(jnp.float32)
    row = jnp.zeros((BINS, CH), jnp.float32)
    for f in range(BINS):
        one = jnp.where(bin_row == f, pick, 0.0).astype(jnp.bfloat16)
        both = x[:, f].reshape(2 * WIN, CH)
        row = row + lax.dot_general(one, both, (((1,), (1,)), ((), ())),
                                    preferred_element_type=jnp.float32)

    def amplitude(values):
        square = values * values
        return jnp.sqrt(square + pltpu.roll(square, WIN, 1)).astype(jnp.bfloat16).astype(jnp.float32)

    own_amp = amplitude(row)
    edge_out[0] = own_amp[0:HALF]
    edge_out[1] = own_amp[BINS - HALF:BINS]
    rows[z] = row.astype(jnp.bfloat16)

    def amplitude_step(i, carry):
        for k in range(4):
            f = HALF + i * 4 + k
            amp[HALF + f] = rounded_amplitude(
                x[0, f].astype(jnp.float32), x[1, f].astype(jnp.float32)).astype(jnp.float32)
        return carry

    lax.fori_loop(0, (BINS - 2 * HALF) // 4, amplitude_step, 0)

    pl.semaphore_wait(barrier, (ROWS - 1) + (COLS - 1) + 2 * ROWS)

    def edge_copy(side, d, slot):
        other = below if side == 0 else above
        return pltpu.make_async_remote_copy(
            src_ref=edge_out.at[side], dst_ref=edge_in.at[1 - side, slot],
            send_sem=es.at[side, d], recv_sem=er.at[side, d],
            device_id=(along_z(d) * COLS + j, other), device_id_type=MESH)

    def row_copy(d, slot):
        return pltpu.make_async_remote_copy(
            src_ref=rows.at[z], dst_ref=rows.at[slot],
            send_sem=zs.at[d], recv_sem=zr.at[d],
            device_id=(along_z(d) * COLS + j, band), device_id_type=MESH)

    def halo_copy(side):
        other = below if side == 0 else above
        return pltpu.make_async_remote_copy(
            src_ref=halo_out.at[side], dst_ref=halo_in.at[1 - side],
            send_sem=hs.at[side], recv_sem=hr.at[side],
            device_id=(rx, other), device_id_type=MESH)

    for d in range(ROWS):
        for side in range(2):
            edge_copy(side, d, z).start()
    for d in (7, 6, 5, 4, 3, 2, 1):
        row_copy(d, z).start()

    @pl.when(band > 0)
    def _():
        halo_copy(0).start()

    @pl.when(band < BANDS - 1)
    def _():
        halo_copy(1).start()

    def whiten_step(i, carry):
        whiten_four(x, amp, white, HALF + i * 4)
        return carry

    lax.fori_loop(0, (BINS - 2 * HALF) // 4, whiten_step, 0)

    for d in range(1, ROWS):
        row_copy(d, lax.rem(z - d + ROWS, ROWS)).wait_recv()
    for d in range(ROWS):
        for side in range(2):
            edge_copy(side, d, lax.rem(z - d + ROWS, ROWS)).wait_recv()

    has_low = (band > 0).astype(jnp.float32)
    has_high = (band < BANDS - 1).astype(jnp.float32)
    for k in range(ROWS):
        values = rows[k].astype(jnp.float32)
        padded = jnp.concatenate(
            [edge_in[0, k] * has_low, amplitude(values), edge_in[1, k] * has_high], axis=0)
        total = padded[0:BINS]
        for offset in range(1, 2 * HALF + 1):
            total = total + padded[offset:offset + BINS]
        smooth = total / (2 * HALF + 1)
        blocks[j, k] = (values / (smooth + 0.1)).astype(jnp.bfloat16)

    def block_copy(d, slot):
        return pltpu.make_async_remote_copy(
            src_ref=blocks.at[j], dst_ref=blocks.at[slot],
            send_sem=js.at[d], recv_sem=jr.at[d],
            device_id=(z * COLS + along_j(d), band), device_id_type=MESH)

    for d in (4, 3, 5, 2, 6, 1, 7):
        block_copy(d, j).start()
    for d in range(1, ROWS):
        row_copy(d, z).wait_send()
    for d in range(ROWS):
        for side in range(2):
            edge_copy(side, d, z).wait_send()
    for d in range(1, COLS):
        block_copy(d, lax.rem(j - d + COLS, COLS)).wait_recv()

    for k in range(ROWS):
        for c in range(COLS):
            source[pl.ds((k * COLS + c) * BINS, BINS), :] = blocks[c, k].astype(jnp.float32)

    def multiply_step(i, carry):
        for k in range(4):
            f = HALF + i * 4 + k
            multiply(coefficients(source, f), white, out_ref, f)
        return carry

    lax.fori_loop(0, (BINS - 2 * HALF) // 4, multiply_step, 0)
    for k in range(HALF):
        left[k] = coefficients(source, k)
        left[HALF + k] = coefficients(source, BINS - HALF + k)

    @pl.when(band == 0)
    def _():
        halo_in[0] = jnp.zeros_like(halo_in[0])

    @pl.when(band > 0)
    def _():
        halo_copy(1).wait_recv()

    for k in range(HALF):
        amp[k] = halo_in[0, k].astype(jnp.float32)
    whiten_four(x, amp, white, 0)
    for k in range(HALF):
        multiply(left[k], white, out_ref, k)

    @pl.when(band == BANDS - 1)
    def _():
        halo_in[1] = jnp.zeros_like(halo_in[1])

    @pl.when(band < BANDS - 1)
    def _():
        halo_copy(0).wait_recv()

    for k in range(HALF):
        amp[BINS + HALF + k] = halo_in[1, k].astype(jnp.float32)
    whiten_four(x, amp, white, BINS - HALF)
    for k in range(HALF):
        multiply(left[HALF + k], white, out_ref, BINS - HALF + k)

    @pl.when(band > 0)
    def _():
        halo_copy(0).wait_send()

    @pl.when(band < BANDS - 1)
    def _():
        halo_copy(1).wait_send()

    for d in range(1, COLS):
        block_copy(d, j).wait_send()


def local(spectra, source_index):
    return pl.pallas_call(
        correlate_kernel,
        out_shape=jax.ShapeDtypeStruct((2, BINS, ROWS * COLS, CH), jnp.bfloat16),
        in_specs=[pl.BlockSpec(memory_space=pltpu.SMEM), pl.BlockSpec(memory_space=pl.ANY)],
        out_specs=pl.BlockSpec(memory_space=pltpu.VMEM),
        scratch_shapes=[
            pltpu.VMEM((2, BINS, WIN, CH), jnp.bfloat16),
            pltpu.VMEM((BINS + 2 * HALF, WIN, CH), jnp.float32),
            pltpu.VMEM((BINS, 2 * WIN, CH), jnp.bfloat16),
            pltpu.VMEM((ROWS * COLS * BINS, 2 * WIN), jnp.float32),
            pltpu.VMEM((2 * HALF, 2 * WIN, 2 * WIN), jnp.bfloat16),
            pltpu.VMEM((2, HALF, WIN, CH), jnp.bfloat16),
            pltpu.VMEM((2, HALF, WIN, CH), jnp.bfloat16),
            pltpu.VMEM((ROWS, BINS, 2 * WIN), jnp.bfloat16),
            pltpu.VMEM((2, HALF, 2 * WIN), jnp.float32),
            pltpu.VMEM((2, ROWS, HALF, 2 * WIN), jnp.float32),
            pltpu.VMEM((COLS, ROWS, BINS, 2 * WIN), jnp.bfloat16),
            pltpu.SemaphoreType.DMA,
            pltpu.SemaphoreType.DMA((ROWS,)),
            pltpu.SemaphoreType.DMA((ROWS,)),
            pltpu.SemaphoreType.DMA((2, ROWS)),
            pltpu.SemaphoreType.DMA((2, ROWS)),
            pltpu.SemaphoreType.DMA((COLS,)),
            pltpu.SemaphoreType.DMA((COLS,)),
            pltpu.SemaphoreType.DMA((2,)),
            pltpu.SemaphoreType.DMA((2,)),
        ],
        compiler_params=pltpu.CompilerParams(collective_id=0, has_side_effects=True),
        name="correlate",
    )(source_index, spectra)


def solution(mesh):
    return jax.shard_map(
        local,
        mesh=mesh,
        in_specs=(P(None, "band", None, "rx"), P()),
        out_specs=P(None, "band", None, "rx"),
        check_vma=False,
    )
```

time: 56.1 us -> 48.2 us (0.86)
  starting transfers between devices: 17.6 us -> 0 us
  Pallas kernels: 35.9 us -> 45.7 us
  other arithmetic: 1.11 us -> 0 us
  local copies, waits for them, and re-layouts: 1.23 us -> 2.26 us
    ppermute x2 -> x0, starting transfers between devices: 17.6 us -> none  [the longest x1 16.3 us: local(): lax.ppermute(edge_amplitude(spectra[:, BINS - HALF:]), 'band', forward)]
    pallas_call x2 -> x1, Pallas kernels: 35.9 us -> 45.7 us  [local(): pl.pallas_call(correlate_kernel, out_shape=jax.ShapeDtypeStruct((2, BINS,...]
    convert_element_type x3 -> x0, other arithmetic: 1.11 us -> none  [the longest x1 1.01 us: edge_amplitude(): values = part.astype(jnp.float32)]
    unnamed x4 -> x1, local copies, waits for them, and re-layouts: 1.23 us -> 2.26 us
  transfers between devices with their start and end apart: 2 -> 0, of which waited for: 0 -> 0; matrix products, arithmetic and copies ran while one was open for 0% -> 0% of each run, Pallas kernels for 57% -> 0%
where the time goes in v2:
time: 48.2 us; the launch traced here: 48 us
  Pallas kernels  45.7 us (95%)
  local copies, waits for them, and re-layouts  2.26 us (5%)
    pallas_call x1, Pallas kernels, local(): pl.pallas_call(correlate_kernel, out_shape=jax.ShapeDtypeStruct((2, BINS,...  45.7 us
    unnamed x1, local copies, waits for them, and re-layouts  2.26 us

profile of v2, /device:TPU:1, one launch (start us, length us, event | category | flops | bytes accessed | tf_op | source)
XLA Modules:
  0.0 48.0 jit_solution(7024481942887881257)
XLA Ops:
  0.0 45.7 %correlate.1 = bf16[2,32,64,128]{3,2,1,0:T(8,128)(2,1)} custom-call(s32[64]{0:T(128)} %src_ref.1, bf16[2,32,64,128]{3,2,1,0:T(8,128)(2,1)} %x_hbm.1), custom_call_target="tpu_custom_call" | custom-call | tf_op jit(solution)/shard_map/correlate/pallas_call | solution.py:247
  45.7 2.3 %copy.4 = bf16[2,32,64,128]{3,2,1,0:T(8,128)(2,1)} copy(bf16[2,32,64,128]{3,2,1,0:T(8,128)(2,1)} %correlate.1) | data formatting | bytes 2097152

commit v3 on v2

--- a/solution.py
+++ b/solution.py
@@ -14,6 +14,7 @@
 ROWS = 8
 COLS = 8
 BANDS = 8
+PART = 4
 MESH = pl.DeviceIdType.MESH
 
 
@@ -50,7 +51,7 @@
 
 
 def correlate_kernel(src_ref, x_hbm, out_ref, x, amp, white, source, left, halo_out, halo_in,
-                     rows, edge_out, edge_in, blocks, xs, zs, zr, es, er, js, jr, hs, hr):
+                     rows, edge_out, edge_in, blocks, xs, zs, zr, es, er, js, jr, ts, tr, hs, hr):
     rx = lax.axis_index("rx")
     band = lax.axis_index("band")
     z = lax.div(rx, COLS)
@@ -61,8 +62,11 @@
     def along_z(d):
         return lax.rem(z + d, ROWS)
 
-    def along_j(d):
-        return lax.rem(j + d, COLS)
+    core = lax.rem(j, 2)
+    partner = j + 1 - 2 * core
+
+    def along_x(d):
+        return lax.rem(j + 2 * d, COLS)
 
     barrier = pltpu.get_barrier_semaphore()
     for d in range(ROWS):
@@ -70,8 +74,9 @@
             pl.semaphore_signal(barrier, inc=1, device_id=(along_z(d) * COLS + j, other), device_id_type=MESH)
     for d in range(1, ROWS):
         pl.semaphore_signal(barrier, inc=1, device_id=(along_z(d) * COLS + j, band), device_id_type=MESH)
-    for d in range(1, COLS):
-        pl.semaphore_signal(barrier, inc=1, device_id=(z * COLS + along_j(d), band), device_id_type=MESH)
+    for d in range(1, COLS // 2):
+        pl.semaphore_signal(barrier, inc=1, device_id=(z * COLS + along_x(d), band), device_id_type=MESH)
+    pl.semaphore_signal(barrier, inc=1, device_id=(z * COLS + partner, band), device_id_type=MESH)
 
     load = pltpu.make_async_copy(x_hbm, x, xs)
     load.start()
@@ -99,9 +104,50 @@
         return jnp.sqrt(square + pltpu.roll(square, WIN, 1)).astype(jnp.bfloat16).astype(jnp.float32)
 
     own_amp = amplitude(row)
-    edge_out[0] = own_amp[0:HALF]
-    edge_out[1] = own_amp[BINS - HALF:BINS]
+    edge_out[0] = own_amp[0:HALF].astype(jnp.bfloat16)
+    edge_out[1] = own_amp[BINS - HALF:BINS].astype(jnp.bfloat16)
     rows[z] = row.astype(jnp.bfloat16)
+
+    pl.semaphore_wait(barrier, (ROWS - 1) + COLS // 2 + 2 * ROWS)
+
+    def edge_copy(side, d, slot):
+        other = below if side == 0 else above
+        return pltpu.make_async_remote_copy(
+            src_ref=edge_out.at[side], dst_ref=edge_in.at[1 - side, slot],
+            send_sem=es.at[side, d], recv_sem=er.at[side, d],
+            device_id=(along_z(d) * COLS + j, other), device_id_type=MESH)
+
+    def row_copy(d, slot):
+        return pltpu.make_async_remote_copy(
+            src_ref=rows.at[z], dst_ref=rows.at[slot],
+            send_sem=zs.at[d], recv_sem=zr.at[d],
+            device_id=(along_z(d) * COLS + j, band), device_id_type=MESH)
+
+    even = lax.rem(band, 2) == 0
+    odd = lax.rem(band, 2) == 1
+
+    def halo_copy(side):
+        other = below if side == 0 else above
+        return pltpu.make_async_remote_copy(
+            src_ref=halo_out.at[side], dst_ref=halo_in.at[1 - side],
+            send_sem=hs.at[side], recv_sem=hr.at[side],
+            device_id=(rx, other), device_id_type=MESH)
+
+    for d in range(ROWS):
+        for side in range(2):
+            edge_copy(side, d, z).start()
+    for d in (7, 6, 5, 4, 3, 2, 1):
+        row_copy(d, z).start()
+
+
+    def start_halo(group):
+        @pl.when(jnp.logical_and(group, band > 0))
+        def _():
+            halo_copy(0).start()
+
+        @pl.when(jnp.logical_and(group, band < BANDS - 1))
+        def _():
+            halo_copy(1).start()
 
     def amplitude_step(i, carry):
         for k in range(4):
@@ -112,47 +158,14 @@
 
     lax.fori_loop(0, (BINS - 2 * HALF) // 4, amplitude_step, 0)
 
-    pl.semaphore_wait(barrier, (ROWS - 1) + (COLS - 1) + 2 * ROWS)
-
-    def edge_copy(side, d, slot):
-        other = below if side == 0 else above
-        return pltpu.make_async_remote_copy(
-            src_ref=edge_out.at[side], dst_ref=edge_in.at[1 - side, slot],
-            send_sem=es.at[side, d], recv_sem=er.at[side, d],
-            device_id=(along_z(d) * COLS + j, other), device_id_type=MESH)
-
-    def row_copy(d, slot):
-        return pltpu.make_async_remote_copy(
-            src_ref=rows.at[z], dst_ref=rows.at[slot],
-            send_sem=zs.at[d], recv_sem=zr.at[d],
-            device_id=(along_z(d) * COLS + j, band), device_id_type=MESH)
-
-    def halo_copy(side):
-        other = below if side == 0 else above
-        return pltpu.make_async_remote_copy(
-            src_ref=halo_out.at[side], dst_ref=halo_in.at[1 - side],
-            send_sem=hs.at[side], recv_sem=hr.at[side],
-            device_id=(rx, other), device_id_type=MESH)
-
-    for d in range(ROWS):
-        for side in range(2):
-            edge_copy(side, d, z).start()
-    for d in (7, 6, 5, 4, 3, 2, 1):
-        row_copy(d, z).start()
-
-    @pl.when(band > 0)
-    def _():
-        halo_copy(0).start()
-
-    @pl.when(band < BANDS - 1)
-    def _():
-        halo_copy(1).start()
-
     def whiten_step(i, carry):
         whiten_four(x, amp, white, HALF + i * 4)
         return carry
 
     lax.fori_loop(0, (BINS - 2 * HALF) // 4, whiten_step, 0)
+
+    start_halo(odd)
+
 
     for d in range(1, ROWS):
         row_copy(d, lax.rem(z - d + ROWS, ROWS)).wait_recv()
@@ -162,43 +175,57 @@
 
     has_low = (band > 0).astype(jnp.float32)
     has_high = (band < BANDS - 1).astype(jnp.float32)
-    for k in range(ROWS):
-        values = rows[k].astype(jnp.float32)
-        padded = jnp.concatenate(
-            [edge_in[0, k] * has_low, amplitude(values), edge_in[1, k] * has_high], axis=0)
-        total = padded[0:BINS]
-        for offset in range(1, 2 * HALF + 1):
-            total = total + padded[offset:offset + BINS]
-        smooth = total / (2 * HALF + 1)
-        blocks[j, k] = (values / (smooth + 0.1)).astype(jnp.bfloat16)
-
-    def block_copy(d, slot):
-        return pltpu.make_async_remote_copy(
-            src_ref=blocks.at[j], dst_ref=blocks.at[slot],
-            send_sem=js.at[d], recv_sem=jr.at[d],
-            device_id=(z * COLS + along_j(d), band), device_id_type=MESH)
-
-    for d in (4, 3, 5, 2, 6, 1, 7):
-        block_copy(d, j).start()
+    def block_copy(d, slot, h):
+        part = pl.ds(h * PART, PART)
+        return pltpu.make_async_remote_copy(
+            src_ref=blocks.at[j, part], dst_ref=blocks.at[slot, part],
+            send_sem=js.at[d, h], recv_sem=jr.at[d, h],
+            device_id=(z * COLS + along_x(d), band), device_id_type=MESH)
+
+    def twin_copy(d, slot, h):
+        part = pl.ds(h * PART, PART)
+        return pltpu.make_async_remote_copy(
+            src_ref=blocks.at[slot, part], dst_ref=blocks.at[slot, part],
+            send_sem=ts.at[d, h], recv_sem=tr.at[d, h],
+            device_id=(z * COLS + partner, band), device_id_type=MESH)
+
+    for h in range(ROWS // PART):
+        for k in range(h * PART, (h + 1) * PART):
+            values = rows[k].astype(jnp.float32)
+            padded = jnp.concatenate(
+                [edge_in[0, k].astype(jnp.float32) * has_low, amplitude(values),
+                 edge_in[1, k].astype(jnp.float32) * has_high], axis=0)
+            total = padded[0:BINS]
+            for offset in range(1, 2 * HALF + 1):
+                total = total + padded[offset:offset + BINS]
+            smooth = total / (2 * HALF + 1)
+            blocks[j, k] = (values / (smooth + 0.1)).astype(jnp.bfloat16)
+        for d in (2, 1, 3):
+            block_copy(d, j, h).start()
+        twin_copy(0, j, h).start()
+    for h in range(ROWS // PART):
+        for d in (1, 3, 2):
+            slot = lax.rem(j - 2 * d + COLS, COLS)
+            block_copy(d, slot, h).wait_recv()
+            twin_copy(d, slot, h).start()
+
+    start_halo(even)
+
     for d in range(1, ROWS):
         row_copy(d, z).wait_send()
     for d in range(ROWS):
         for side in range(2):
             edge_copy(side, d, z).wait_send()
-    for d in range(1, COLS):
-        block_copy(d, lax.rem(j - d + COLS, COLS)).wait_recv()
+    for h in range(ROWS // PART):
+        for d in (0, 1, 3, 2):
+            twin_copy(d, lax.rem(partner - 2 * d + COLS, COLS), h).wait_recv()
 
     for k in range(ROWS):
         for c in range(COLS):
             source[pl.ds((k * COLS + c) * BINS, BINS), :] = blocks[c, k].astype(jnp.float32)
 
-    def multiply_step(i, carry):
-        for k in range(4):
-            f = HALF + i * 4 + k
-            multiply(coefficients(source, f), white, out_ref, f)
-        return carry
-
-    lax.fori_loop(0, (BINS - 2 * HALF) // 4, multiply_step, 0)
+    for f in range(HALF, BINS - HALF):
+        multiply(coefficients(source, f), white, out_ref, f)
     for k in range(HALF):
         left[k] = coefficients(source, k)
         left[HALF + k] = coefficients(source, BINS - HALF + k)
@@ -239,14 +266,17 @@
     def _():
         halo_copy(1).wait_send()
 
-    for d in range(1, COLS):
-        block_copy(d, j).wait_send()
+    for h in range(ROWS // PART):
+        for d in range(1, COLS // 2):
+            block_copy(d, j, h).wait_send()
+        for d in range(COLS // 2):
+            twin_copy(d, lax.rem(j - 2 * d + COLS, COLS), h).wait_send()
 
 
 def local(spectra, source_index):
     return pl.pallas_call(
         correlate_kernel,
-        out_shape=jax.ShapeDtypeStruct((2, BINS, ROWS * COLS, CH), jnp.bfloat16),
+        out_shape=pltpu.VMEM((2, BINS, ROWS * COLS, CH), jnp.bfloat16),
         in_specs=[pl.BlockSpec(memory_space=pltpu.SMEM), pl.BlockSpec(memory_space=pl.ANY)],
         out_specs=pl.BlockSpec(memory_space=pltpu.VMEM),
         scratch_shapes=[
@@ -258,16 +288,18 @@
             pltpu.VMEM((2, HALF, WIN, CH), jnp.bfloat16),
             pltpu.VMEM((2, HALF, WIN, CH), jnp.bfloat16),
             pltpu.VMEM((ROWS, BINS, 2 * WIN), jnp.bfloat16),
-            pltpu.VMEM((2, HALF, 2 * WIN), jnp.float32),
-            pltpu.VMEM((2, ROWS, HALF, 2 * WIN), jnp.float32),
+            pltpu.VMEM((2, HALF, 2 * WIN), jnp.bfloat16),
+            pltpu.VMEM((2, ROWS, HALF, 2 * WIN), jnp.bfloat16),
             pltpu.VMEM((COLS, ROWS, BINS, 2 * WIN), jnp.bfloat16),
             pltpu.SemaphoreType.DMA,
             pltpu.SemaphoreType.DMA((ROWS,)),
             pltpu.SemaphoreType.DMA((ROWS,)),
             pltpu.SemaphoreType.DMA((2, ROWS)),
             pltpu.SemaphoreType.DMA((2, ROWS)),
-            pltpu.SemaphoreType.DMA((COLS,)),
-            pltpu.SemaphoreType.DMA((COLS,)),
+            pltpu.SemaphoreType.DMA((COLS // 2, ROWS // PART)),
+            pltpu.SemaphoreType.DMA((COLS // 2, ROWS // PART)),
+            pltpu.SemaphoreType.DMA((COLS // 2, ROWS // PART)),
+            pltpu.SemaphoreType.DMA((COLS // 2, ROWS // PART)),
             pltpu.SemaphoreType.DMA((2,)),
             pltpu.SemaphoreType.DMA((2,)),
         ],

time: 48.2 us -> 39.7 us (0.82)
  the two profiles are of different devices: /device:TPU:1 before, /device:TPU:40 now
where the time goes in v3:
time: 39.7 us; the launch traced here: 39.6 us
  Pallas kernels  38.6 us (97%)
  local copies, waits for them, and re-layouts  0.97 us (2%)
    pallas_call x1, Pallas kernels, local(): pl.pallas_call(correlate_kernel, out_shape=pltpu.VMEM((2, BINS, ROWS * CO...  38.6 us
    unnamed x1, local copies, waits for them, and re-layouts  0.97 us

profile of v3, /device:TPU:40, one launch (start us, length us, event | category | flops | bytes accessed | tf_op | source)
XLA Modules:
  0.0 39.6 jit_solution(4407660041411537560)
XLA Ops:
  0.0 38.6 %correlate.1 = bf16[2,32,64,128]{3,2,1,0:T(8,128)(2,1)S(1)} custom-call(s32[64]{0:T(128)} %src_ref.1, bf16[2,32,64,128]{3,2,1,0:T(8,128)(2,1)} %x_hbm.1), custom_call_target="tpu_custom_call" | custom-call | tf_op jit(solution)/shard_map/correlate/pallas_call | solution.py:277
  38.6 1.0 %copy.4 = bf16[2,32,64,128]{3,2,1,0:T(8,128)(2,1)} copy(bf16[2,32,64,128]{3,2,1,0:T(8,128)(2,1)S(1)} %correlate.1) | data formatting | bytes 2097152

commit v4 on v3

--- a/solution.py
+++ b/solution.py
@@ -69,9 +69,18 @@
         return lax.rem(j + 2 * d, COLS)
 
     barrier = pltpu.get_barrier_semaphore()
-    for d in range(ROWS):
-        for other in (above, below):
+    def greet(other):
+        for d in range(ROWS):
             pl.semaphore_signal(barrier, inc=1, device_id=(along_z(d) * COLS + j, other), device_id_type=MESH)
+
+    @pl.when(band > 0)
+    def _():
+        greet(below)
+
+    @pl.when(band < BANDS - 1)
+    def _():
+        greet(above)
+
     for d in range(1, ROWS):
         pl.semaphore_signal(barrier, inc=1, device_id=(along_z(d) * COLS + j, band), device_id_type=MESH)
     for d in range(1, COLS // 2):
@@ -108,7 +117,8 @@
     edge_out[1] = own_amp[BINS - HALF:BINS].astype(jnp.bfloat16)
     rows[z] = row.astype(jnp.bfloat16)
 
-    pl.semaphore_wait(barrier, (ROWS - 1) + COLS // 2 + 2 * ROWS)
+    beside = jnp.where(band > 0, ROWS, 0) + jnp.where(band < BANDS - 1, ROWS, 0)
+    pl.semaphore_wait(barrier, (ROWS - 1) + COLS // 2 + beside)
 
     def edge_copy(side, d, slot):
         other = below if side == 0 else above
@@ -133,12 +143,18 @@
             send_sem=hs.at[side], recv_sem=hr.at[side],
             device_id=(rx, other), device_id_type=MESH)
 
-    for d in range(ROWS):
-        for side in range(2):
-            edge_copy(side, d, z).start()
+    @pl.when(band > 0)
+    def _():
+        for d in range(ROWS):
+            edge_copy(0, d, z).start()
+
+    @pl.when(band < BANDS - 1)
+    def _():
+        for d in range(ROWS):
+            edge_copy(1, d, z).start()
+
     for d in (7, 6, 5, 4, 3, 2, 1):
         row_copy(d, z).start()
-
 
     def start_halo(group):
         @pl.when(jnp.logical_and(group, band > 0))
@@ -166,15 +182,29 @@
 
     start_halo(odd)
 
-
     for d in range(1, ROWS):
         row_copy(d, lax.rem(z - d + ROWS, ROWS)).wait_recv()
-    for d in range(ROWS):
-        for side in range(2):
-            edge_copy(side, d, lax.rem(z - d + ROWS, ROWS)).wait_recv()
-
-    has_low = (band > 0).astype(jnp.float32)
-    has_high = (band < BANDS - 1).astype(jnp.float32)
+
+    @pl.when(band > 0)
+    def _():
+        for d in range(ROWS):
+            edge_copy(1, d, lax.rem(z - d + ROWS, ROWS)).wait_recv()
+
+    @pl.when(band == 0)
+    def _():
+        edge_in[0] = jnp.zeros_like(edge_in[0])
+
+    @pl.when(band < BANDS - 1)
+    def _():
+        for d in range(ROWS):
+            edge_copy(0, d, lax.rem(z - d + ROWS, ROWS)).wait_recv()
+
+    @pl.when(band == BANDS - 1)
+    def _():
+        edge_in[1] = jnp.zeros_like(edge_in[1])
+
+    start_halo(even)
+
     def block_copy(d, slot, h):
         part = pl.ds(h * PART, PART)
         return pltpu.make_async_remote_copy(
@@ -193,8 +223,8 @@
         for k in range(h * PART, (h + 1) * PART):
             values = rows[k].astype(jnp.float32)
             padded = jnp.concatenate(
-                [edge_in[0, k].astype(jnp.float32) * has_low, amplitude(values),
-                 edge_in[1, k].astype(jnp.float32) * has_high], axis=0)
+                [edge_in[0, k].astype(jnp.float32), amplitude(values),
+                 edge_in[1, k].astype(jnp.float32)], axis=0)
             total = padded[0:BINS]
             for offset in range(1, 2 * HALF + 1):
                 total = total + padded[offset:offset + BINS]
@@ -209,13 +239,19 @@
             block_copy(d, slot, h).wait_recv()
             twin_copy(d, slot, h).start()
 
-    start_halo(even)
-
     for d in range(1, ROWS):
         row_copy(d, z).wait_send()
-    for d in range(ROWS):
-        for side in range(2):
-            edge_copy(side, d, z).wait_send()
+
+    @pl.when(band > 0)
+    def _():
+        for d in range(ROWS):
+            edge_copy(0, d, z).wait_send()
+
+    @pl.when(band < BANDS - 1)
+    def _():
+        for d in range(ROWS):
+            edge_copy(1, d, z).wait_send()
+
     for h in range(ROWS // PART):
         for d in (0, 1, 3, 2):
             twin_copy(d, lax.rem(partner - 2 * d + COLS, COLS), h).wait_recv()

time: 39.7 us -> 36.9 us (0.929)
  the two profiles are of different devices: /device:TPU:40 before, /device:TPU:1 now
where the time goes in v4:
time: 36.9 us; the launch traced here: 36.7 us
  Pallas kernels  35.7 us (97%)
  local copies, waits for them, and re-layouts  0.97 us (3%)
    pallas_call x1, Pallas kernels, local(): pl.pallas_call(correlate_kernel, out_shape=pltpu.VMEM((2, BINS, ROWS * CO...  35.7 us
    unnamed x1, local copies, waits for them, and re-layouts  0.97 us

profile of v4, /device:TPU:1, one launch (start us, length us, event | category | flops | bytes accessed | tf_op | source)
XLA Modules:
  0.0 36.7 jit_solution(3707497188297377870)
XLA Ops:
  0.0 35.7 %correlate.1 = bf16[2,32,64,128]{3,2,1,0:T(8,128)(2,1)S(1)} custom-call(s32[64]{0:T(128)} %src_ref.1, bf16[2,32,64,128]{3,2,1,0:T(8,128)(2,1)} %x_hbm.1), custom_call_target="tpu_custom_call" | custom-call | tf_op jit(solution)/shard_map/correlate/pallas_call | solution.py:313
  35.7 1.0 %copy.4 = bf16[2,32,64,128]{3,2,1,0:T(8,128)(2,1)} copy(bf16[2,32,64,128]{3,2,1,0:T(8,128)(2,1)S(1)} %correlate.1) | data formatting | bytes 2097152

commit v5 on v4

--- a/solution.py
+++ b/solution.py
@@ -143,18 +143,37 @@
             send_sem=hs.at[side], recv_sem=hr.at[side],
             device_id=(rx, other), device_id_type=MESH)
 
-    @pl.when(band > 0)
-    def _():
-        for d in range(ROWS):
-            edge_copy(0, d, z).start()
-
-    @pl.when(band < BANDS - 1)
-    def _():
-        for d in range(ROWS):
-            edge_copy(1, d, z).start()
-
-    for d in (7, 6, 5, 4, 3, 2, 1):
-        row_copy(d, z).start()
+    def start_edges():
+        @pl.when(band > 0)
+        def _():
+            for d in range(ROWS):
+                edge_copy(0, d, z).start()
+
+        @pl.when(band < BANDS - 1)
+        def _():
+            for d in range(ROWS):
+                edge_copy(1, d, z).start()
+
+    def start_rows():
+        for d in (7, 6, 5, 4, 3, 2, 1):
+            row_copy(d, z).start()
+
+    @pl.when(odd)
+    def _():
+        start_edges()
+
+    @pl.when(even)
+    def _():
+        start_rows()
+
+    @pl.when(odd)
+    def _():
+        start_rows()
+
+    @pl.when(even)
+    def _():
+        start_edges()
+
 
     def start_halo(group):
         @pl.when(jnp.logical_and(group, band > 0))
@@ -252,13 +271,20 @@
         for d in range(ROWS):
             edge_copy(1, d, z).wait_send()
 
+    def widen(slot, h):
+        for k in range(h * PART, (h + 1) * PART):
+            at = pl.multiple_of((k * COLS + slot) * BINS, BINS)
+            source[pl.ds(at, BINS), :] = blocks[slot, k].astype(jnp.float32)
+
+    for h in range(ROWS // PART):
+        for d in range(COLS // 2):
+            widen(lax.rem(j - 2 * d + COLS, COLS), h)
     for h in range(ROWS // PART):
         for d in (0, 1, 3, 2):
-            twin_copy(d, lax.rem(partner - 2 * d + COLS, COLS), h).wait_recv()
-
-    for k in range(ROWS):
-        for c in range(COLS):
-            source[pl.ds((k * COLS + c) * BINS, BINS), :] = blocks[c, k].astype(jnp.float32)
+            slot = lax.rem(partner - 2 * d + COLS, COLS)
+            twin_copy(d, slot, h).wait_recv()
+            widen(slot, h)
+
 
     for f in range(HALF, BINS - HALF):
         multiply(coefficients(source, f), white, out_ref, f)

time: 36.9 us -> 36.8 us (level)
  no operation moved by 1% of the time
where the time goes in v5:
time: 36.8 us; the launch traced here: 36.6 us
  Pallas kernels  35.6 us (97%)
  local copies, waits for them, and re-layouts  0.97 us (3%)
    pallas_call x1, Pallas kernels, local(): pl.pallas_call(correlate_kernel, out_shape=pltpu.VMEM((2, BINS, ROWS * CO...  35.6 us
    unnamed x1, local copies, waits for them, and re-layouts  0.97 us

profile of v5, /device:TPU:1, one launch (start us, length us, event | category | flops | bytes accessed | tf_op | source)
XLA Modules:
  0.0 36.6 jit_solution(15378680793101275177)
XLA Ops:
  0.0 35.6 %correlate.1 = bf16[2,32,64,128]{3,2,1,0:T(8,128)(2,1)S(1)} custom-call(s32[64]{0:T(128)} %src_ref.1, bf16[2,32,64,128]{3,2,1,0:T(8,128)(2,1)} %x_hbm.1), custom_call_target="tpu_custom_call" | custom-call | tf_op jit(solution)/shard_map/correlate/pallas_call | solution.py:339
  35.6 1.0 %copy.4 = bf16[2,32,64,128]{3,2,1,0:T(8,128)(2,1)} copy(bf16[2,32,64,128]{3,2,1,0:T(8,128)(2,1)S(1)} %correlate.1) | data formatting | bytes 2097152
